TPU v7x, 32 devices: a whole 2x2x4 slice. The times are simulated.
32 devices in a mesh: ep: 32 (over z, y, x, core), kv: 1.
Axes of the slice: x: 2, y: 2, z: 4, core: 2. Of those that a mesh axis runs over, the one named last changes fastest.
Arguments:
- tokens: bfloat16 [4096, 2560], P('ep'), may hold values from -6 to 6
- routes: int32 [4096, 6], P('ep'), may hold values from 0 to 15, all different within a row; in each aligned block of 128 rows (0 to 127, 128 to 255, ...) at most 64 rows name the same one
- route_weights: float32 [4096, 6], P('ep'), may hold values from 0.05 to 0.4
- w_gate: bfloat16 [32, 2560, 768], P('ep', None, 'kv'), may hold values from -0.125 to 0.125
- w_up: bfloat16 [32, 2560, 768], P('ep', None, 'kv'), may hold values from -0.125 to 0.125
- w_down: bfloat16 [32, 768, 2560], P('ep', 'kv'), may hold values from -0.15625 to 0.15625
- queries: bfloat16 [32, 2560], P('ep')
- key_cache: bfloat16 [32, 1024, 512], P('ep', 'kv')
- value_cache: bfloat16 [32, 1024, 512], P('ep', 'kv'), may hold values from -6 to 6
- lengths: int32 [32], P('ep'), may hold values from 1 to 1024, as said below
Outputs:
- moe_out: bfloat16 [4096, 2560], P('ep')
- attn_out: bfloat16 [32, 2560], P('ep')
Inputs may be any that keep to these rules, and one draw needn't show every extreme that they name: `routes`: each row names 6 different experts; among the rows of one index of ep no expert is named by more than 64 rows, a bound that some block reaches of them. Request r uses cache positions 0 to lengths[r] - 1; some request has exactly 1024.
All inputs are finite; a program needn't handle non-finite values.
Results may differ from a plain program's by a relative error of at most 0.015.
Values may be sent and summed in bfloat16 or wider, within the bound.
A program may use at most 128 MiB of HBM per device.

v0:
```python
import math

import jax
import jax.numpy as jnp
from jax import lax
from jax.sharding import PartitionSpec as P

QUERY_HEADS = 20
KEY_VALUE_HEADS = 4
HEAD_SIZE = 128


floor_score = -1e30


def attend(queries, key_cache, value_cache, lengths):
    request_list = queries.shape[0]
    window_length = key_cache.shape[1]
    heads_of_queries = queries.reshape(
        request_list, KEY_VALUE_HEADS, QUERY_HEADS // KEY_VALUE_HEADS, HEAD_SIZE
    )
    heads_of_keys = key_cache.reshape(request_list, window_length, KEY_VALUE_HEADS, HEAD_SIZE)
    heads_of_values = value_cache.reshape(request_list, window_length, KEY_VALUE_HEADS, HEAD_SIZE)
    scores = jnp.einsum(
        "rgjd,rcgd->rgjc", heads_of_queries, heads_of_keys, preferred_element_type=jnp.float32
    )
    scores = scores * (1.0 / math.sqrt(HEAD_SIZE))
    position = lax.axis_index("kv") * window_length + jnp.arange(window_length, dtype=jnp.int32)
    valid = (position[None, :] < lengths[:, None])[:, None, None, :]
    scores = jnp.where(valid, scores, floor_score)
    top = lax.pmax(jnp.max(scores, axis=-1), "kv")
    weights = jnp.where(valid, jnp.exp(scores - top[..., None]), 0.0)
    local_total = jnp.sum(weights, axis=-1)
    local_mixed = jnp.einsum(
        "rgjc,rcgd->rgjd",
        weights.astype(jnp.bfloat16),
        heads_of_values,
        preferred_element_type=jnp.float32,
    )
    total, mixed = lax.psum((local_total, local_mixed), "kv")
    return (
        (mixed / total[..., None])
        .reshape(request_list, QUERY_HEADS * HEAD_SIZE)
        .astype(jnp.bfloat16)
    )


def expert_math(flat_rows, gate_part, up_part, down_part):
    gate_act = jnp.dot(flat_rows, gate_part, preferred_element_type=jnp.float32)
    up_act = jnp.dot(flat_rows, up_part, preferred_element_type=jnp.float32)
    hidden = (jax.nn.silu(gate_act) * up_act).astype(jnp.bfloat16)
    return jnp.dot(hidden, down_part, preferred_element_type=jnp.float32)


def shards(
    tokens, routes, route_weights, w_gate, w_up, w_down, queries, key_cache, value_cache, lengths
):
    tok = tokens.shape[0]
    width = tokens.shape[1]
    topk = routes.shape[1]
    halves = lax.axis_size("ep")
    shares = lax.axis_size("kv")
    experts = halves // 2
    cap = tok * topk * 4 // (3 * experts)
    share_cap = cap // shares
    kv_index = lax.axis_index("kv")
    chosen = routes.reshape(-1)
    onehot = (chosen[:, None] == jnp.arange(experts, dtype=jnp.int32)[None, :]).astype(jnp.int32)
    before = jnp.cumsum(onehot, axis=0) - onehot
    slot = jnp.sum(before * onehot, axis=1)
    owner = jnp.arange(tok * topk, dtype=jnp.int32) // topk
    pick = jnp.full((experts * cap,), tok, jnp.int32).at[chosen * cap + slot].set(owner)
    padded = jnp.concatenate([tokens, jnp.zeros((1, width), tokens.dtype)], axis=0)
    outgoing = padded[pick].reshape(experts, cap, width)
    arrived = lax.all_to_all(
        jnp.repeat(outgoing, 2, axis=0), "ep", split_axis=0, concat_axis=0, tiled=True
    )
    flat_rows = arrived.reshape(halves * cap, width)
    partial_out = expert_math(flat_rows, w_gate[0], w_up[0], w_down[0]).reshape(halves, cap, width)
    half_out = lax.psum_scatter(
        partial_out.astype(jnp.bfloat16), "kv", scatter_dimension=1, tiled=True
    )
    back = lax.all_to_all(half_out, "ep", split_axis=0, concat_axis=0, tiled=True)
    table = back.reshape(halves * share_cap, width)
    local_slot = slot - kv_index * share_cap
    held = (local_slot >= 0) & (local_slot < share_cap)
    safe_slot = jnp.where(held, local_slot, 0)
    first_row = 2 * chosen * share_cap + safe_slot
    both = table[first_row].astype(jnp.float32) + table[first_row + share_cap].astype(jnp.float32)
    factor = jnp.where(held, route_weights.reshape(-1), 0.0)
    weighted = both * factor[:, None]
    summed = jnp.sum(weighted.reshape(tok, topk, width), axis=1)
    moe_out = lax.psum(summed.astype(jnp.bfloat16), "kv")
    attn_out = attend(queries, key_cache, value_cache, lengths)
    return (moe_out, attn_out)


def solution(mesh):
    return jax.shard_map(
        shards,
        mesh=mesh,
        in_specs=(
            P("ep", None),
            P("ep", None),
            P("ep", None),
            P("ep", None, "kv"),
            P("ep", None, "kv"),
            P("ep", "kv", None),
            P("ep", None),
            P("ep", "kv", None),
            P("ep", "kv", None),
            P("ep"),
        ),
        out_specs=(P("ep", None), P("ep", None)),
        check_vma=False,
    )
```

profile of v0, /device:TPU:9, one launch (start us, length us, event | category | flops | bytes accessed | tf_op | source)
XLA Modules:
  0.0 574.3 jit_solution(10123560300485315516)
XLA Ops:
  0.6 0.8 copy.16
  1.4 0.1 eq.29
  1.6 0.1 eq.25
  1.7 0.7 broadcast_multiply_fusion
  2.4 1.7 reduce-window.6
  4.1 0.3 slice_reduce_fusion
  4.4 0.1 copy.15
  4.5 0.1 mul.63
  4.7 0.1 copy.19
  4.8 0.1 mul.69
  4.9 0.1 fusion.15
  5.1 3.4 scatter_custom_fusion
  8.5 1.1 concatenate.3
  9.6 6.3 %gather_fusion = bf16[1024,2560]{1,0:T(8,128)(2,1)} fusion(bf16[129,2560]{1,0:T(8,128)(2,1)S(1)} %concatenate.3, s32[1024]{0:T(1024)S(1)} %fusion.19), kind=kCustom, calls=%fused_computation | custom fusion | bytes 10489856 | tf_op jit(solution)/shard_map/gather | solution.py:74
  15.9 7.9 %broadcast_in_dim.46 = bf16[16,2,64,2560]{3,2,1,0:T(8,128)(2,1)} broadcast(bf16[16,64,2560]{2,1,0:T(8,128)(2,1)} %bitcast.44), dimensions={0,2,3} | broadcast | bytes 15728640 | tf_op jit(solution)/shard_map/broadcast_in_dim | solution.py:76
  23.8 0.0 copy-start.4
  23.8 233.9 %all_to_all.10 = bf16[32,64,2560]{2,1,0:T(8,128)(2,1)S(1)} all-to-all(bf16[32,64,2560]{2,1,0:T(8,128)(2,1)} %bitcast.43), channel_id=1, replica_groups=mesh['ep'=32,'kv'=1] {'ep'}, dimensions={0} | all-to-all | bytes 20971520 | tf_op jit(solution)/shard_map/all_to_all | solution.py:75
  257.7 0.0 copy-done.4
  257.7 0.0 copy-start.5
  257.7 10.1 %fusion.3 = f32[2048,768]{1,0:T(8,128)} fusion(bf16[2048,2560]{1,0:T(8,128)(2,1)S(1)} %bitcast.45, bf16[1,2560,768]{2,1,0:T(8,128)(2,1)S(1)} %copy-done.4), kind=kOutput, calls=%fused_computation.11 | convolution fusion | flops 8053063680 | bytes 20709376 | tf_op jit(solution)/shard_map/dot_general | solution.py:49
  267.8 0.0 copy-done.5
  267.9 0.0 copy-start.6
  267.9 11.1 %multiply_convert_fusion = bf16[2048,768]{1,0:T(8,128)(2,1)S(1)} fusion(f32[2048,768]{1,0:T(8,128)} %fusion.3, bf16[2048,2560]{1,0:T(8,128)(2,1)S(1)} %bitcast.46, bf16[1,2560,768]{2,1,0:T(8,128)(2,1)S(1)} %copy-done.5), kind=kOutput, calls=%fused_computation.8 | convolution fusion | flops 8062500864 | bytes 23855104 | tf_op jit(solution)/shard_map/dot_general | solution.py:50
  278.9 0.0 copy-done.6
  278.9 11.0 %convolution_convert_fusion = bf16[32,64,2560]{2,1,0:T(8,128)(2,1)} fusion(bf16[32,64,768]{2,1,0:T(8,128)(2,1)S(1)} %bitcast.48, bf16[1,768,2560]{2,1,0:T(8,128)(2,1)S(1)} %copy-done.6), kind=kOutput, calls=%fused_computation.6 | convolution fusion | flops 8058306560 | bytes 17563648 | tf_op jit(solution)/shard_map/dot_general | solution.py:52
  289.9 0.0 copy-start.3
  289.9 0.0 copy-start
  289.9 0.0 copy-start.2
  289.9 0.0 copy-start.1
  289.9 5.0 all-to-all-start.1
  294.9 0.2 and.30
  295.1 0.0 copy-done.3
  295.1 0.1 copy.20
  295.9 0.0 copy-done
  295.9 0.3 reshape.216
  296.2 0.0 copy-done.2
  296.2 0.0 copy-done.1
  296.2 0.3 reshape.217
  296.6 0.4 fusion.8
  296.9 0.2 fusion.27
  297.1 0.3 fusion.9
  297.5 0.6 convert_element_type.53
  298.2 223.2 %all-to-all-done.1 = bf16[32,64,2560]{2,1,0:T(8,128)(2,1)} async-done(((bf16[32,64,2560]{2,1,0:T(8,128)(2,1)}), bf16[32,64,2560]{2,1,0:T(8,128)(2,1)}, u32[]{:S(2)}, u32[]{:S(2)}) %all-to-all-start.1) | async-done | bytes 10485792 | tf_op jit(solution)/shard_map/all_to_all | solution.py:83
  521.3 13.7 %gather_fusion.1 = bf16[768,2560]{1,0:T(8,128)(2,1)} fusion(bf16[2048,2560]{1,0:T(8,128)(2,1)} %bitcast.9, s32[1024]{0:T(1024)S(1)} %get-tuple-element.9), kind=kCustom, calls=%fused_computation.1 | custom fusion | bytes 7867392 | tf_op jit(solution)/shard_map/gather | solution.py:89
  535.0 13.7 %gather_fusion.2 = bf16[768,2560]{1,0:T(8,128)(2,1)} fusion(bf16[2048,2560]{1,0:T(8,128)(2,1)} %bitcast.9, s32[1024]{0:T(1024)S(1)} %get-tuple-element.8), kind=kCustom, calls=%fused_computation.2 | custom fusion | bytes 7867392 | tf_op jit(solution)/shard_map/gather | solution.py:89
  548.7 7.5 %convert_add_fusion = f32[768,2560]{1,0:T(8,128)} fusion(bf16[768,2560]{1,0:T(8,128)(2,1)} %gather_fusion.2, bf16[768,2560]{1,0:T(8,128)(2,1)} %gather_fusion.1), kind=kLoop, calls=%fused_computation.7 | loop fusion | flops 5898240 | bytes 15728640 | tf_op jit(solution)/shard_map/add | solution.py:89
  556.2 9.2 %add.111 = f32[128,6,2560]{2,1,0:T(8,128)} reshape(f32[768,2560]{1,0:T(8,128)} %convert_add_fusion) | data formatting | bytes 15728640 | tf_op jit(solution)/shard_map/add | solution.py:89
  565.5 8.8 %multiply_reduce_fusion = bf16[128,2560]{1,0:T(8,128)(2,1)} fusion(f32[128,6,2560]{2,1,0:T(8,128)} %add.111, f32[128,6]{1,0:T(8,128)S(1)} %broadcast_select_fusion), kind=kLoop, calls=%fused_computation.5 | loop fusion | flops 3604480 | bytes 8522752 | tf_op jit(solution)/shard_map/reduce_sum | solution.py:92
  (12 shorter events, 0.2 us)
Async XLA Ops:
  23.8 233.9 %copy-start.4 = (bf16[1,2560,768]{2,1,0:T(8,128)(2,1)S(1)}, bf16[1,2560,768]{2,1,0:T(8,128)(2,1)}, u32[]{:S(2)}) copy-start(bf16[1,2560,768]{2,1,0:T(8,128)(2,1)} %param.13) | copy-start | bytes 11796484
  257.7 10.1 %copy-start.5 = (bf16[1,2560,768]{2,1,0:T(8,128)(2,1)S(1)}, bf16[1,2560,768]{2,1,0:T(8,128)(2,1)}, u32[]{:S(2)}) copy-start(bf16[1,2560,768]{2,1,0:T(8,128)(2,1)} %param.14) | copy-start | bytes 11796484
  267.9 11.1 %copy-start.6 = (bf16[1,768,2560]{2,1,0:T(8,128)(2,1)S(1)}, bf16[1,768,2560]{2,1,0:T(8,128)(2,1)}, u32[]{:S(2)}) copy-start(bf16[1,768,2560]{2,1,0:T(8,128)(2,1)} %param.15) | copy-start | bytes 11796484
  289.9 5.2 copy-start.3
  289.9 5.9 %copy-start = (bf16[1,1024,512]{2,1,0:T(8,128)(2,1)S(1)}, bf16[1,1024,512]{2,1,0:T(8,128)(2,1)}, u32[]{:S(2)}) copy-start(bf16[1,1024,512]{2,1,0:T(8,128)(2,1)} %param.17) | copy-start | bytes 3145732
  289.9 6.2 %copy-start.2 = (bf16[1,2560]{1,0:T(2,128)(2,1)S(1)}, bf16[1,2560]{1,0:T(2,128)(2,1)}, u32[]{:S(2)}) copy-start(bf16[1,2560]{1,0:T(2,128)(2,1)} %param.16) | copy-start | bytes 15364
  289.9 6.3 %copy-start.1 = (bf16[1,1024,512]{2,1,0:T(8,128)(2,1)S(1)}, bf16[1,1024,512]{2,1,0:T(8,128)(2,1)}, u32[]{:S(2)}) copy-start(bf16[1,1024,512]{2,1,0:T(8,128)(2,1)} %param.18) | copy-start | bytes 3145732
  289.9 231.4 %all-to-all-start.1 = ((bf16[32,64,2560]{2,1,0:T(8,128)(2,1)}), bf16[32,64,2560]{2,1,0:T(8,128)(2,1)}, u32[]{:S(2)}, u32[]{:S(2)}) async-start(bf16[32,64,2560]{2,1,0:T(8,128)(2,1)} %convolution_convert_fusion), calls=%async_computation.1 | async-start | bytes 20971520 | tf_op jit(solution)/shard_map/all_to_all | solution.py:83
where the time goes:
time: 582 us; the launch traced here: 574 us
  blocking collectives  234 us (40%)
  waiting for transfers between devices  223 us (38%)
  local copies, waits for them, and re-layouts  58.7 us (10%)
  matrix products  32.9 us (6%)
  other arithmetic  19.2 us (3%)
    all_to_all x1, blocking collectives, shards(): lax.all_to_all(jnp.repeat(outgoing, 2, axis=0), 'ep', split_axis=0, conca...  234 us
    all_to_all x1, waiting for transfers between devices, shards(): lax.all_to_all(half_out, 'ep', split_axis=0, concat_axis=0, tiled=True)  223 us
    gather x1, local copies, waits for them, and re-layouts, shards(): table[first_row].astype(jnp.float32)  13.7 us
    gather x1, local copies, waits for them, and re-layouts, shards(): table[first_row + share_cap].astype(jnp.float32)  13.7 us
  transfers between devices with their start and end apart: 1, of which 1 were waited for; matrix products, arithmetic and copies ran while one was open for 0% of the time, Pallas kernels for 0%

commit v1 on v0

--- a/solution.py
+++ b/solution.py
@@ -52,9 +52,39 @@
     return jnp.dot(hidden, down_part, preferred_element_type=jnp.float32)
 
 
+def expert_gathered(tokens, routes, route_weights, w_gate, w_up, w_down):
+    tok, width = tokens.shape
+    topk = routes.shape[1]
+    halves = lax.axis_size("ep")
+    cap = tok * topk * 4 // (3 * (halves // 2))
+    expert = lax.axis_index("ep") // 2
+    plan = jnp.concatenate([routes.astype(jnp.float32), route_weights], axis=1)
+    plans = lax.all_gather(plan, "ep", axis=0)
+    gathered = lax.all_gather(tokens, "ep", axis=0)
+    match = plans[:, :, :topk] == expert.astype(jnp.float32)
+    routed = jnp.any(match, axis=2)
+    factor = jnp.sum(jnp.where(match, plans[:, :, topk:], 0.0), axis=2)
+    earlier = jnp.triu(jnp.ones((tok, tok), jnp.bfloat16), 1)
+    slot = jnp.dot(routed.astype(jnp.bfloat16), earlier, preferred_element_type=jnp.float32)
+    slot = jnp.where(routed, slot.astype(jnp.int32), -1)
+    chosen = slot[:, None, :] == jnp.arange(cap, dtype=jnp.int32)[None, :, None]
+    pick = chosen.astype(jnp.bfloat16)
+    scale = jnp.sum(jnp.where(chosen, factor[:, None, :], 0.0), axis=2)
+    rows = jnp.einsum("bst,btd->bsd", pick, gathered, preferred_element_type=jnp.float32)
+    rows = rows.astype(jnp.bfloat16).reshape(halves * cap, width)
+    half_out = expert_math(rows, w_gate[0], w_up[0], w_down[0])
+    weighted = (half_out.reshape(halves, cap, width) * scale[:, :, None]).astype(jnp.bfloat16)
+    spread = jnp.einsum("bst,bsd->btd", pick, weighted, preferred_element_type=jnp.float32)
+    spread = spread.astype(jnp.bfloat16).reshape(halves * tok, width)
+    return lax.psum_scatter(spread, "ep", scatter_dimension=0, tiled=True)
+
+
 def shards(
     tokens, routes, route_weights, w_gate, w_up, w_down, queries, key_cache, value_cache, lengths
 ):
+    if lax.axis_size("kv") == 1:
+        moe_out = expert_gathered(tokens, routes, route_weights, w_gate, w_up, w_down)
+        return (moe_out, attend(queries, key_cache, value_cache, lengths))
     tok = tokens.shape[0]
     width = tokens.shape[1]
     topk = routes.shape[1]

time: 582 us -> 431 us (0.74); the launches traced: 574 us -> 429 us
  blocking collectives: 234 us -> 37 us
  waiting for transfers between devices: 223 us -> 323 us
  local copies, waits for them, and re-layouts: 58.7 us -> 2.48 us
  matrix products: 32.9 us -> 50.3 us
  other arithmetic: 19.2 us -> 2.18 us
  between operations: 1.48 us -> 14.8 us
    all_to_all x1 -> x0, blocking collectives: 234 us -> none  [shards(): lax.all_to_all(jnp.repeat(outgoing, 2, axis=0), 'ep', split_axis=0, conca...]
    all_to_all x1 -> x0, waiting for transfers between devices: 223 us -> none  [shards(): lax.all_to_all(half_out, 'ep', split_axis=0, concat_axis=0, tiled=True)]
    reduce_scatter x0 -> x1, waiting for transfers between devices: none -> 223 us  [expert_gathered(): return lax.psum_scatter(spread, 'ep', scatter_dimension=0, tiled=True)]
    all_gather x0 -> x1, waiting for transfers between devices: none -> 99.1 us  [expert_gathered(): gathered = lax.all_gather(tokens, 'ep', axis=0)]
    all_gather x0 -> x1, blocking collectives: none -> 37 us  [expert_gathered(): plans = lax.all_gather(plan, 'ep', axis=0)]
    gather x3 -> x0, local copies, waits for them, and re-layouts: 33.7 us -> none  [the longest x1 13.7 us: shards(): table[first_row].astype(jnp.float32)]
    dot_general x1 -> x3, matrix products: 11 us -> 28.3 us  [the longest x1 19.6 us: expert_gathered(): jnp.einsum('bst,bsd->btd', pick, weighted, preferred_element_type=jnp.flo...]
    add x1 -> x0, local copies, waits for them, and re-layouts: 9.24 us -> none  [shards(): table[first_row].astype(jnp.float32)]
  transfers between devices with their start and end apart: 1 -> 2, of which waited for: 1 -> 2; matrix products, arithmetic and copies ran while one was open for 0% -> 1% of each run, Pallas kernels for 0% -> 0%
where the time goes in v1:
time: 431 us; the launch traced here: 429 us
  waiting for transfers between devices  323 us (75%)
  matrix products  50.3 us (12%)
  blocking collectives  37 us (9%)
  between operations  14.8 us (3%)
    reduce_scatter x1, waiting for transfers between devices, expert_gathered(): return lax.psum_scatter(spread, 'ep', scatter_dimension=0, tiled=True)  223 us
    all_gather x1, waiting for transfers between devices, expert_gathered(): gathered = lax.all_gather(tokens, 'ep', axis=0)  99.1 us
    all_gather x1, blocking collectives, expert_gathered(): plans = lax.all_gather(plan, 'ep', axis=0)  37 us
    dot_general x1, matrix products, expert_gathered(): jnp.einsum('bst,bsd->btd', pick, weighted, preferred_element_type=jnp.flo...  19.6 us
    dot_general x1, matrix products, expert_math(): gate_act = jnp.dot(flat_rows, gate_part, preferred_element_type=jnp.float32)  11.1 us
    dot_general x1, matrix products, expert_math(): up_act = jnp.dot(flat_rows, up_part, preferred_element_type=jnp.float32)  10.1 us
  transfers between devices with their start and end apart: 2, of which 2 were waited for; matrix products, arithmetic and copies ran while one was open for 1% of the time, Pallas kernels for 0%

profile of v1, /device:TPU:9, one launch (start us, length us, event | category | flops | bytes accessed | tf_op | source)
XLA Modules:
  0.0 429.4 jit_solution(17649948842857447866)
XLA Ops:
  7.2 0.0 all-gather.4.cloned.1.call-start
  7.2 0.7 all-gather.4.cloned.1.call-update
  7.9 0.0 reduce-scatter.2.cloned.1.call-start
  8.0 0.7 convert_element_type.41
  8.6 0.7 pad_maximum_fusion
  9.3 37.0 %all-gather = f32[4096,12]{0,1:T(8,128)S(1)} all-gather(f32[128,12]{0,1:T(8,128)S(1)} %pad_maximum_fusion), channel_id=2, replica_groups=mesh['ep'=32,'kv'=1] {'ep'}, dimensions={0}, use_global_device_ids=true | all-gather | bytes 202752 | tf_op jit(solution)/shard_map/all_gather | solution.py:62
  46.3 0.1 copy.16
  46.4 0.1 fusion.13
  46.6 0.5 select_reduce_fusion
  47.1 99.1 %all-gather.4.cloned.1.call-done = bf16[4096,2560]{1,0:T(8,128)(2,1)} async-done(((bf16[128,2560]{1,0:T(8,128)(2,1)}), bf16[4096,2560]{1,0:T(8,128)(2,1)}) %all-gather.4.cloned.1.call-update) | async-done | bytes 20971536 | tf_op jit(solution)/shard_map/all_gather | solution.py:63
  146.1 8.5 %convolution_convert_fusion.1 = bf16[32,64,2560]{2,1,0:T(8,128)(2,1)S(1)} fusion(bf16[32,128,2560]{2,1,0:T(8,128)(2,1)} %bitcast.31, s32[32,128]{1,0:T(8,128)S(1)} %fusion.13), kind=kOutput, calls=%fused_computation.5 | convolution fusion | flops 1347682304 | bytes 31473664 | tf_op jit(solution)/shard_map/bst,btd->bsd/dot_general | solution.py:73
  154.7 0.0 copy-start.3
  154.7 11.1 %fusion.7 = f32[2048,768]{1,0:T(8,128)S(1)} fusion(bf16[2048,2560]{1,0:T(8,128)(2,1)S(1)} %bitcast.33, bf16[1,2560,768]{2,1,0:T(8,128)(2,1)} %param.13), kind=kOutput, calls=%fused_computation.9 | convolution fusion | flops 8053063680 | bytes 20709376 | tf_op jit(solution)/shard_map/dot_general | solution.py:49
  165.8 0.0 copy-done.3
  165.9 10.1 %multiply_convert_fusion.2 = bf16[2048,768]{1,0:T(8,128)(2,1)} fusion(f32[2048,768]{1,0:T(8,128)S(1)} %fusion.7, bf16[2048,2560]{1,0:T(8,128)(2,1)S(1)} %bitcast.34, bf16[1,2560,768]{2,1,0:T(8,128)(2,1)S(1)} %copy-done.3), kind=kOutput, calls=%fused_computation.6 | convolution fusion | flops 8062500864 | bytes 23855104 | tf_op jit(solution)/shard_map/dot_general | solution.py:50
  176.0 19.6 %convolution_convert_fusion = bf16[32,128,2560]{2,1,0:T(8,128)(2,1)} fusion(f32[32,64]{1,0:T(8,128)S(1)} %select_reduce_fusion, bf16[32,64,768]{2,1,0:T(8,128)(2,1)} %bitcast.37, bf16[1,768,2560]{2,1,0:T(8,128)(2,1)} %param.15, s32[32,128]{1,0:T(8,128)S(1)} %fusion.13), kind=kOutput, calls=%fused_computation.2 | convolution fusion | flops 9416474624 | bytes 28073984 | tf_op jit(solution)/shard_map/bst,bsd->btd/dot_general | solution.py:77
  195.6 0.0 copy-start
  195.6 0.0 copy-start.2
  195.6 0.0 copy-start.1
  195.6 0.0 reduce-scatter.2.cloned.1.call-update
  195.7 1.2 copy-done
  196.8 0.3 reshape.81
  197.1 0.0 copy-done.2
  197.2 0.0 copy-done.1
  197.2 0.3 reshape.80
  198.2 0.4 fusion.12
  198.5 0.2 fusion.28
  198.7 0.3 fusion.14
  199.1 0.6 convert_element_type.50
  199.7 222.8 %reduce-scatter.2.cloned.1.call-done = bf16[128,2560]{1,0:T(8,128)(2,1)} async-done(((bf16[4096,2560]{1,0:T(8,128)(2,1)}), bf16[128,2560]{1,0:T(8,128)(2,1)}) %reduce-scatter.2.cloned.1.call-update) | async-done | bytes 655376 | tf_op jit(solution)/shard_map/reduce_scatter | solution.py:79
  (6 shorter events, 0.1 us)
Async XLA Ops:
  7.2 139.0 %all-gather.4.cloned.1.call-start = ((), (), s32[]{:S(2)}) async-start(), calls=%async_computation.2 | async-start | bytes 21626880 | tf_op jit(solution)/shard_map/all_gather | solution.py:63
  7.9 414.7 %reduce-scatter.2.cloned.1.call-start = ((), (), s32[]{:S(2)}) async-start(), calls=%async_computation.1 | async-start | bytes 21626880 | tf_op jit(solution)/shard_map/reduce_scatter | solution.py:79
  154.7 11.2 %copy-start.3 = (bf16[1,2560,768]{2,1,0:T(8,128)(2,1)S(1)}, bf16[1,2560,768]{2,1,0:T(8,128)(2,1)}, u32[]{:S(2)}) copy-start(bf16[1,2560,768]{2,1,0:T(8,128)(2,1)} %param.14) | copy-start | bytes 11796484
  195.6 1.2 copy-start
  195.6 1.5 copy-start.2
  195.6 1.6 copy-start.1
Sparse Core Ops, SparseCore 0:
  10.9 135.2 all-gather.3
  195.8 226.7 reduce-scatter.1

commit v2 on v0

--- a/solution.py
+++ b/solution.py
@@ -1,8 +1,11 @@
+import functools
 import math
 
 import jax
 import jax.numpy as jnp
 from jax import lax
+from jax.experimental import pallas as pl
+from jax.experimental.pallas import tpu as pltpu
 from jax.sharding import PartitionSpec as P
 
 QUERY_HEADS = 20
@@ -52,9 +55,244 @@
     return jnp.dot(hidden, down_part, preferred_element_type=jnp.float32)
 
 
+MESH = pl.DeviceIdType.MESH
+PLANE = ((0, 0), (1, 0), (0, 1), (1, 1))
+
+
+def place(nz):
+    me = lax.axis_index("ep")
+    return me // 8, (me // 4) % 2, (me // 2) % 2, me % 2
+
+
+def index_of(z, y, x, core):
+    return ((z * 2 + y) * 2 + x) * 2 + core
+
+
+def flip(value, bit):
+    return 1 - value if bit else value
+
+
+def greet(peers):
+    barrier = pltpu.get_barrier_semaphore()
+    for peer in peers:
+        pl.semaphore_signal(barrier, inc=1, device_id={"ep": peer}, device_id_type=MESH)
+    pl.semaphore_wait(barrier, len(peers))
+
+
+def push(src, dst, send_sem, recv_sem, peer):
+    copy = pltpu.make_async_remote_copy(
+        src_ref=src,
+        dst_ref=dst,
+        send_sem=send_sem,
+        recv_sem=recv_sem,
+        device_id={"ep": peer},
+        device_id_type=MESH,
+    )
+    copy.start()
+    return copy
+
+
+def neighbours(nz):
+    z, y, x, core = place(nz)
+    plane = [index_of(z, flip(y, dy), flip(x, dx), core) for dx, dy in PLANE]
+    partner = index_of(z, y, x, 1 - core)
+    ahead = [index_of((z + step) % nz, y, x, core) for step in range(nz)]
+    behind = [index_of((z + nz - step) % nz, y, x, core) for step in range(nz)]
+    experts = [(z * 2 + flip(y, dy)) * 2 + flip(x, dx) for dx, dy in PLANE]
+    return plane, partner, ahead, behind, experts
+
+
+def arrival_order(nz):
+    return [0] + sorted(range(1, nz), key=lambda step: min(step, nz - step))
+
+
+def dispatch_kernel(
+    nz, cap, tokens, plan, rows, plans, line, picked,
+    line_send, line_recv, plan_send, plan_recv, plane_send, plane_recv, core_send, core_recv,
+):
+    plane, partner, ahead, behind, experts = neighbours(nz)
+    tok = tokens.shape[0]
+    greet(plane[1:] + [partner] + ahead[1:])
+    line_copies, plan_copies = [None] * nz, [None] * nz
+    for step in arrival_order(nz)[1:]:
+        plan_copies[step] = push(
+            plan, plans.at[step], plan_send.at[step], plan_recv.at[step], ahead[step]
+        )
+        line_copies[step] = push(
+            tokens, line.at[step], line_send.at[step], line_recv.at[step], ahead[step]
+        )
+    plans[0] = plan[...]
+    row_of = lax.broadcasted_iota(jnp.int32, (cap, tok), 0).astype(jnp.float32)
+    plane_copies, core_copies, local_copies = {}, {}, []
+
+    def forward(step):
+        for p in range(1, 4):
+            plane_copies[p, step].wait_recv()
+            core_copies[p, step] = push(
+                rows.at[0, p, step], rows.at[1, p, step],
+                core_send.at[p, step], core_recv.at[p, step], partner,
+            )
+
+    last = None
+    for step in arrival_order(nz):
+        if step:
+            plan_copies[step].wait_recv()
+            line_copies[step].wait_recv()
+        block = line.at[step] if step else tokens
+        for p in (3, 1, 2, 0):
+            slots = plans[step, pl.ds(experts[p], 1), :]
+            pick = jnp.where(row_of == slots, 1.0, 0.0).astype(jnp.bfloat16)
+            picked[p, step] = jnp.dot(
+                pick, block[...], preferred_element_type=jnp.float32
+            ).astype(jnp.bfloat16)
+            if p:
+                plane_copies[p, step] = push(
+                    picked.at[p, step], rows.at[0, p, step],
+                    plane_send.at[p, step], plane_recv.at[p, step], plane[p],
+                )
+            else:
+                core_copies[p, step] = push(
+                    picked.at[p, step], rows.at[1, p, step],
+                    core_send.at[p, step], core_recv.at[p, step], partner,
+                )
+                copy = pltpu.make_async_copy(
+                    picked.at[p, step], rows.at[0, p, step], plane_send.at[p, step]
+                )
+                copy.start()
+                local_copies.append(copy)
+        if last is not None:
+            forward(last)
+        last = step
+    forward(last)
+    for copy in local_copies:
+        copy.wait()
+    for copy in plan_copies[1:] + line_copies[1:] + list(plane_copies.values()):
+        copy.wait_send()
+    for copy in core_copies.values():
+        copy.wait()
+
+
+def combine_kernel(
+    nz, cap, half_out, plans, out, own, other, back, partial, sums,
+    own_sem, core_send, core_recv, plane_send, plane_recv, line_send, line_recv,
+):
+    plane, partner, ahead, behind, experts = neighbours(nz)
+    tok = out.shape[0]
+    greet(plane[1:] + [partner] + behind[1:])
+    order = arrival_order(nz)[1:][::-1] + [0]
+    core_copies, own_copies, plane_copies, line_copies = {}, {}, {}, {}
+    for step in order:
+        for p in (3, 1, 2, 0):
+            core_copies[p, step] = push(
+                half_out.at[1, p, step], other.at[p, step],
+                core_send.at[p, step], core_recv.at[p, step], partner,
+            )
+            own_copies[p, step] = pltpu.make_async_copy(
+                half_out.at[0, p, step], own.at[p, step], own_sem.at[p, step]
+            )
+            own_copies[p, step].start()
+    for step in order:
+        for p in (3, 1, 2, 0):
+            core_copies[p, step].wait_recv()
+            own_copies[p, step].wait()
+            both = own[p, step].astype(jnp.float32) + other[p, step].astype(jnp.float32)
+            sums[p, step] = both.astype(jnp.bfloat16)
+            if p:
+                plane_copies[p, step] = push(
+                    sums.at[p, step], back.at[p, step],
+                    plane_send.at[p, step], plane_recv.at[p, step], plane[p],
+                )
+    row_of = lax.broadcasted_iota(jnp.int32, (cap, tok), 0).astype(jnp.float32)
+    total = None
+    for step in order:
+        total = jnp.zeros((tok, out.shape[1]), jnp.float32)
+        for p in (0, 2, 1, 3):
+            if p:
+                plane_copies[p, step].wait_recv()
+            slots = plans[step, pl.ds(experts[p], 1), :]
+            factors = plans[step, pl.ds(experts[p] + 4 * nz, 1), :]
+            spread = jnp.where(row_of == slots, factors, 0.0).T
+            high = spread.astype(jnp.bfloat16)
+            low = (spread - high.astype(jnp.float32)).astype(jnp.bfloat16)
+            values = back[p, step] if p else sums[p, step]
+            total += jnp.dot(high, values, preferred_element_type=jnp.float32)
+            total += jnp.dot(low, values, preferred_element_type=jnp.float32)
+        if step:
+            partial[0, step] = total.astype(jnp.bfloat16)
+            line_copies[step] = push(
+                partial.at[0, step], partial.at[1, step],
+                line_send.at[step], line_recv.at[step], behind[step],
+            )
+    for step in order[:-1]:
+        line_copies[step].wait_recv()
+        total += partial[1, step].astype(jnp.float32)
+    out[...] = total.astype(out.dtype)
+    for copies in (core_copies, plane_copies, line_copies):
+        for copy in copies.values():
+            copy.wait_send()
+
+
+def expert_lines(tokens, routes, route_weights, w_gate, w_up, w_down):
+    tok, width = tokens.shape
+    topk = routes.shape[1]
+    halves = lax.axis_size("ep")
+    experts = halves // 2
+    nz = halves // 8
+    cap = tok * topk * 4 // (3 * experts)
+    match = routes[None, :, :] == jnp.arange(experts, dtype=jnp.int32)[:, None, None]
+    routed = jnp.any(match, axis=2)
+    factor = jnp.sum(jnp.where(match, route_weights[None, :, :], 0.0), axis=2)
+    earlier = jnp.triu(jnp.ones((tok, tok), jnp.bfloat16), 1)
+    slot = jnp.dot(routed.astype(jnp.bfloat16), earlier, preferred_element_type=jnp.float32)
+    plan = jnp.concatenate([jnp.where(routed, slot, -1.0), factor], axis=0)
+    vmem, anywhere = pl.BlockSpec(memory_space=pltpu.VMEM), pl.BlockSpec(memory_space=pl.ANY)
+    dma = pltpu.SemaphoreType.DMA
+    rows, plans = pl.pallas_call(
+        functools.partial(dispatch_kernel, nz, cap),
+        out_shape=(
+            jax.ShapeDtypeStruct((2, 4, nz, cap, width), jnp.bfloat16),
+            jax.ShapeDtypeStruct((nz, 2 * experts, tok), jnp.float32),
+        ),
+        in_specs=[vmem, vmem],
+        out_specs=(anywhere, vmem),
+        scratch_shapes=[
+            pltpu.VMEM((nz, tok, width), jnp.bfloat16),
+            pltpu.VMEM((4, nz, cap, width), jnp.bfloat16),
+            dma((nz,)), dma((nz,)), dma((nz,)), dma((nz,)),
+            dma((4, nz)), dma((4, nz)), dma((4, nz)), dma((4, nz)),
+        ],
+        compiler_params=pltpu.CompilerParams(
+            collective_id=0, has_side_effects=True, vmem_limit_bytes=40 << 20
+        ),
+    )(tokens, plan)
+    half_out = expert_math(rows.reshape(halves * cap, width), w_gate[0], w_up[0], w_down[0])
+    half_out = half_out.astype(jnp.bfloat16).reshape(2, 4, nz, cap, width)
+    return pl.pallas_call(
+        functools.partial(combine_kernel, nz, cap),
+        out_shape=jax.ShapeDtypeStruct((tok, width), jnp.bfloat16),
+        in_specs=[anywhere, vmem],
+        out_specs=vmem,
+        scratch_shapes=[
+            pltpu.VMEM((4, nz, cap, width), jnp.bfloat16),
+            pltpu.VMEM((4, nz, cap, width), jnp.bfloat16),
+            pltpu.VMEM((4, nz, cap, width), jnp.bfloat16),
+            pltpu.VMEM((2, nz, tok, width), jnp.bfloat16),
+            pltpu.VMEM((4, nz, cap, width), jnp.bfloat16),
+            dma((4, nz)), dma((4, nz)), dma((4, nz)), dma((4, nz)), dma((4, nz)),
+            dma((nz,)), dma((nz,)),
+        ],
+        compiler_params=pltpu.CompilerParams(
+            collective_id=1, has_side_effects=True, vmem_limit_bytes=48 << 20
+        ),
+    )(half_out, plans)
+
+
 def shards(
     tokens, routes, route_weights, w_gate, w_up, w_down, queries, key_cache, value_cache, lengths
 ):
+    if lax.axis_size("kv") == 1:
+        moe_out = expert_lines(tokens, routes, route_weights, w_gate, w_up, w_down)
+        return (moe_out, attend(queries, key_cache, value_cache, lengths))
     tok = tokens.shape[0]
     width = tokens.shape[1]
     topk = routes.shape[1]

time: 582 us -> 217 us (0.37)
  blocking collectives: 234 us -> 0 us
  waiting for transfers between devices: 223 us -> 0 us
  Pallas kernels: 0 us -> 161 us
  local copies, waits for them, and re-layouts: 58.7 us -> 8 us
  other arithmetic: 19.2 us -> 1.68 us
  matrix products: 32.9 us -> 42.3 us
    all_to_all x1 -> x0, blocking collectives: 234 us -> none  [shards(): lax.all_to_all(jnp.repeat(outgoing, 2, axis=0), 'ep', split_axis=0, conca...]
    all_to_all x1 -> x0, waiting for transfers between devices: 223 us -> none  [shards(): lax.all_to_all(half_out, 'ep', split_axis=0, concat_axis=0, tiled=True)]
    pallas_call x0 -> x2, Pallas kernels: none -> 161 us  [the longest x1 94.4 us: expert_lines(): pl.pallas_call(functools.partial(combine_kernel, nz, cap), out_shape=jax....]
    gather x3 -> x0, local copies, waits for them, and re-layouts: 33.7 us -> none  [the longest x1 13.7 us: shards(): table[first_row].astype(jnp.float32)]
    dot_general x1, matrix products: 11 us -> 28.8 us  [expert_math(): return jnp.dot(hidden, down_part, preferred_element_type=jnp.float32)]
    dot_general x1, matrix products: 11.1 us -> 0.13 us  [expert_lines(): jnp.dot(routed.astype(jnp.bfloat16), earlier, preferred_element_type=jnp....]
    add x1 -> x0, local copies, waits for them, and re-layouts: 9.24 us -> none  [shards(): table[first_row].astype(jnp.float32)]
    reduce_sum x2 -> x1, other arithmetic: 8.92 us -> 0.72 us  [expert_lines(): factor = jnp.sum(jnp.where(match, route_weights[None, :, :], 0.0), axis=2)]
  transfers between devices with their start and end apart: 1 -> 0, of which waited for: 1 -> 0; matrix products, arithmetic and copies ran while one was open for 0% -> 0% of each run, Pallas kernels for 0% -> 0%
where the time goes in v2:
time: 217 us; the launch traced here: 215 us
  Pallas kernels  161 us (74%)
  matrix products  42.3 us (19%)
  local copies, waits for them, and re-layouts  8 us (4%)
    pallas_call x1, Pallas kernels, expert_lines(): pl.pallas_call(functools.partial(combine_kernel, nz, cap), out_shape=jax....  94.4 us
    pallas_call x1, Pallas kernels, expert_lines(): pl.pallas_call(functools.partial(dispatch_kernel, nz, cap), out_shape=(ja...  66.9 us
    dot_general x1, matrix products, expert_math(): return jnp.dot(hidden, down_part, preferred_element_type=jnp.float32)  28.8 us
    dot_general x1, matrix products, expert_math(): gate_act = jnp.dot(flat_rows, gate_part, preferred_element_type=jnp.float32)  11.4 us
    unnamed x11, local copies, waits for them, and re-layouts  5.92 us

profile of v2, /device:TPU:9, one launch (start us, length us, event | category | flops | bytes accessed | tf_op | source)
XLA Modules:
  0.0 214.6 jit_solution(4040039276912757717)
XLA Ops:
  0.6 0.7 select_reduce_fusion
  1.3 0.7 fusion.16
  2.0 0.1 convolution_select_fusion
  2.2 0.0 copy-start
  2.2 1.1 copy-done
  3.3 66.9 %shard_map.113 = (bf16[2,4,4,64,2560]{4,3,2,1,0:T(8,128)(2,1)S(1)}, f32[4,32,128]{2,1,0:T(8,128)S(1)}) custom-call(bf16[128,2560]{1,0:T(8,128)(2,1)S(1)} %copy-done, f32[32,128]{1,0:T(8,128)S(1)} %pad_maximum_fusion.plan), custom_call_target="tpu_custom_call" | custom-call | tf_op jit(solution)/shard_map/pallas_call | solution.py:250
  70.2 0.0 copy-start.1
  70.2 4.0 %copy-done.1 = bf16[2,4,4,64,2560]{4,3,2,1,0:T(8,128)(2,1)} copy-done((bf16[2,4,4,64,2560]{4,3,2,1,0:T(8,128)(2,1)}, bf16[2,4,4,64,2560]{4,3,2,1,0:T(8,128)(2,1)S(1)}, u32[]{:S(2)}) %copy-start.1) | copy-done | bytes 10485784
  74.2 11.4 %fusion.4 = f32[2048,768]{1,0:T(8,128)} fusion(bf16[2048,2560]{1,0:T(8,128)(2,1)S(1)} %bitcast.20, bf16[1,2560,768]{2,1,0:T(8,128)(2,1)} %param.13), kind=kOutput, calls=%fused_computation.5 | convolution fusion | flops 8053063680 | bytes 20709376 | tf_op jit(solution)/shard_map/dot_general | solution.py:52
  85.6 28.8 %convolution_convert_fusion = bf16[2048,2560]{1,0:T(8,128)(2,1)} fusion(f32[2048,768]{1,0:T(8,128)} %fusion.4, bf16[2048,2560]{1,0:T(8,128)(2,1)} %bitcast.21, bf16[1,768,2560]{2,1,0:T(8,128)(2,1)} %param.15, bf16[1,2560,768]{2,1,0:T(8,128)(2,1)} %param.14), kind=kOutput, calls=%fused_computation.1 | convolution fusion | flops 16120807424 | bytes 35127296 | tf_op jit(solution)/shard_map/dot_general | solution.py:55
  114.4 0.0 copy-start.2
  114.4 0.0 copy-start.4
  114.5 0.0 copy-start.3
  114.5 94.4 %shard_map.114 = bf16[128,2560]{1,0:T(8,128)(2,1)S(1)} custom-call(bf16[2,4,4,64,2560]{4,3,2,1,0:T(8,128)(2,1)} %bitcast.22, f32[4,32,128]{2,1,0:T(8,128)S(1)} %get-tuple-element.5.plans), custom_call_target="tpu_custom_call" | custom-call | tf_op jit(solution)/shard_map/pallas_call | solution.py:270
  208.9 0.0 copy-done.2
  208.9 1.1 reshape.78
  210.0 0.0 copy-done.4
  210.1 0.0 copy-done.3
  210.1 0.3 reshape.77
  211.0 0.4 fusion.10
  211.4 0.2 fusion.23
  211.6 1.6 fusion.11
  213.2 0.6 convert_element_type.29
  213.8 0.8 copy.28
  (4 shorter events, 0.1 us)
Async XLA Ops:
  2.2 1.1 copy-start
  70.2 4.0 %copy-start.1 = (bf16[2,4,4,64,2560]{4,3,2,1,0:T(8,128)(2,1)}, bf16[2,4,4,64,2560]{4,3,2,1,0:T(8,128)(2,1)S(1)}, u32[]{:S(2)}) copy-start(bf16[2,4,4,64,2560]{4,3,2,1,0:T(8,128)(2,1)S(1)} %get-tuple-element.4) | copy-start | bytes 31457284
  114.4 94.4 %copy-start.2 = (bf16[1,1024,512]{2,1,0:T(8,128)(2,1)S(1)}, bf16[1,1024,512]{2,1,0:T(8,128)(2,1)}, u32[]{:S(2)}) copy-start(bf16[1,1024,512]{2,1,0:T(8,128)(2,1)} %param.18) | copy-start | bytes 3145732
  114.4 95.6 %copy-start.4 = (bf16[1,2560]{1,0:T(2,128)(2,1)S(1)}, bf16[1,2560]{1,0:T(2,128)(2,1)}, u32[]{:S(2)}) copy-start(bf16[1,2560]{1,0:T(2,128)(2,1)} %param.16) | copy-start | bytes 15364
  114.5 95.6 %copy-start.3 = (bf16[1,1024,512]{2,1,0:T(8,128)(2,1)S(1)}, bf16[1,1024,512]{2,1,0:T(8,128)(2,1)}, u32[]{:S(2)}) copy-start(bf16[1,1024,512]{2,1,0:T(8,128)(2,1)} %param.17) | copy-start | bytes 3145732

commit v3 on v0

--- a/solution.py
+++ b/solution.py
@@ -1,8 +1,11 @@
+import functools
 import math
 
 import jax
 import jax.numpy as jnp
 from jax import lax
+from jax.experimental import pallas as pl
+from jax.experimental.pallas import tpu as pltpu
 from jax.sharding import PartitionSpec as P
 
 QUERY_HEADS = 20
@@ -52,9 +55,270 @@
     return jnp.dot(hidden, down_part, preferred_element_type=jnp.float32)
 
 
+MESH = pl.DeviceIdType.MESH
+PLANE = ((0, 0), (1, 0), (0, 1), (1, 1))
+
+
+def place(nz):
+    me = lax.axis_index("ep")
+    return me // 8, (me // 4) % 2, (me // 2) % 2, me % 2
+
+
+def index_of(z, y, x, core):
+    return ((z * 2 + y) * 2 + x) * 2 + core
+
+
+def flip(value, bit):
+    return 1 - value if bit else value
+
+
+def greet(peers):
+    barrier = pltpu.get_barrier_semaphore()
+    for peer in peers:
+        pl.semaphore_signal(barrier, inc=1, device_id={"ep": peer}, device_id_type=MESH)
+    pl.semaphore_wait(barrier, len(peers))
+
+
+def push(src, dst, send_sem, recv_sem, peer):
+    copy = pltpu.make_async_remote_copy(
+        src_ref=src,
+        dst_ref=dst,
+        send_sem=send_sem,
+        recv_sem=recv_sem,
+        device_id={"ep": peer},
+        device_id_type=MESH,
+    )
+    copy.start()
+    return copy
+
+
+def neighbours(nz):
+    z, y, x, core = place(nz)
+    plane = [index_of(z, flip(y, dy), flip(x, dx), core) for dx, dy in PLANE]
+    partner = index_of(z, y, x, 1 - core)
+    line = [index_of(mirror(z, step), y, x, core) for step in range(nz)]
+    experts = [(z * 2 + flip(y, dy)) * 2 + flip(x, dx) for dx, dy in PLANE]
+    return plane, partner, line, experts
+
+
+def mirror(z, step):
+    value, unit = 0, 1
+    while unit <= step:
+        value += unit * flip((z // unit) % 2, (step // unit) % 2)
+        unit *= 2
+    return value + (z // unit) * unit
+
+
+def experts_kernel(
+    nz, cap, tokens, plan, w_gate, w_up, w_down, out,
+    plans, line, picked, rows, hidden, result, other, back, partial, gate_w, up_w, down_w,
+    weight_sem, plan_send, plan_recv, line_send, line_recv, plane_send, plane_recv,
+    core_send, core_recv, pair_send, pair_recv, back_send, back_recv, home_send, home_recv,
+):
+    plane, partner, peers, experts = neighbours(nz)
+    tok, width = tokens.shape
+    units = w_gate.shape[1]
+    row_of = lax.broadcasted_iota(jnp.int32, (cap, tok), 0).astype(jnp.float32)
+    far = (3, 1, 2)
+    copies = {}
+
+    def chunk(core, p):
+        return pl.ds((core * 4 + p) * cap, cap)
+
+    def half(core):
+        return pl.ds(core * 4 * cap, 4 * cap)
+
+    def spread_line(step):
+        copies["plan", step] = push(
+            plan, plans.at[step], plan_send.at[step], plan_recv.at[step], peers[step]
+        )
+        copies["line", step] = push(
+            tokens, line.at[step - 1], line_send.at[step], line_recv.at[step], peers[step]
+        )
+
+    def dispatch(step):
+        if step:
+            copies["plan", step].wait_recv()
+            copies["line", step].wait_recv()
+        block = line.at[step - 1] if step else tokens
+        for p in far + (0,):
+            slots = plans[step, pl.ds(experts[p], 1), :]
+            pick = jnp.where(row_of == slots, 1.0, 0.0).astype(jnp.bfloat16)
+            value = jnp.dot(pick, block[...], preferred_element_type=jnp.float32)
+            value = value.astype(jnp.bfloat16)
+            if p:
+                picked[step, p - 1] = value
+                copies["plane", step, p] = push(
+                    picked.at[step, p - 1], rows.at[step, chunk(0, p)],
+                    plane_send.at[step, p], plane_recv.at[step, p], plane[p],
+                )
+            else:
+                rows[step, chunk(0, 0)] = value
+                pass_on(step, 0)
+
+    def pass_on(step, p):
+        copies["core", step, p] = push(
+            rows.at[step, chunk(0, p)], rows.at[step, chunk(1, p)],
+            core_send.at[step, p], core_recv.at[step, p], partner,
+        )
+
+    def forward(step):
+        for p in (1, 2, 3):
+            copies["plane", step, p].wait_recv()
+            pass_on(step, p)
+
+    def compute(step):
+        for p in range(4):
+            copies["core", step, p].wait_recv()
+        if step == 0:
+            for copy in weights:
+                copy.wait()
+        block = rows.at[step]
+        wide = 256
+
+        def first(tile, carry):
+            at = pl.ds(pl.multiple_of(tile * wide, wide), wide)
+            gate = jnp.dot(block[...], gate_w[:, at], preferred_element_type=jnp.float32)
+            up = jnp.dot(block[...], up_w[:, at], preferred_element_type=jnp.float32)
+            hidden[:, at] = (gate / (1.0 + jnp.exp(-gate)) * up).astype(jnp.bfloat16)
+            return carry
+
+        lax.fori_loop(0, units // wide, first, 0)
+        broad = 512
+
+        def second(tile, carry):
+            at = pl.ds(pl.multiple_of(tile * broad, broad), broad)
+            value = jnp.dot(hidden[...], down_w[:, at], preferred_element_type=jnp.float32)
+            result[step, :, at] = value.astype(jnp.bfloat16)
+            return carry
+
+        lax.fori_loop(0, width // broad, second, 0)
+        copies["pair", step] = push(
+            result.at[step, half(1)], other.at[step],
+            pair_send.at[step], pair_recv.at[step], partner,
+        )
+
+    def finish(step):
+        copies["pair", step].wait_recv()
+        for p in far + (0,):
+            at = pl.ds(p * cap, cap)
+            both = result[step, at].astype(jnp.float32) + other[step, at].astype(jnp.float32)
+            if p:
+                result[step, at] = both.astype(jnp.bfloat16)
+                copies["back", step, p] = push(
+                    result.at[step, at], back.at[step, at],
+                    back_send.at[step, p], back_recv.at[step, p], plane[p],
+                )
+            else:
+                back[step, at] = both.astype(jnp.bfloat16)
+
+    def expand(step):
+        spread = []
+        for p in range(4):
+            if p:
+                copies["back", step, p].wait_recv()
+            slots = plans[step, pl.ds(experts[p], 1), :]
+            factors = plans[step, pl.ds(experts[p] + 4 * nz, 1), :]
+            spread.append(jnp.where(row_of == slots, factors, 0.0))
+        spread = jnp.concatenate(spread, axis=0).T
+        high = spread.astype(jnp.bfloat16)
+        low = (spread - high.astype(jnp.float32)).astype(jnp.bfloat16)
+        total = jnp.dot(high, back[step], preferred_element_type=jnp.float32)
+        total += jnp.dot(low, back[step], preferred_element_type=jnp.float32)
+        if step:
+            partial[0, step - 1] = total.astype(jnp.bfloat16)
+            copies["home", step] = push(
+                partial.at[0, step - 1], partial.at[1, step - 1],
+                home_send.at[step], home_recv.at[step], peers[step],
+            )
+        return total
+
+    weights = [
+        pltpu.make_async_copy(source, target, weight_sem.at[i])
+        for i, (source, target) in enumerate(((w_gate, gate_w), (w_up, up_w), (w_down, down_w)))
+    ]
+    greet(plane[1:] + [partner] + peers[1:])
+    for step in range(1, nz - 1):
+        spread_line(step)
+    for copy in weights:
+        copy.start()
+    plans[0] = plan[...]
+    dispatch(0)
+    forward(0)
+    dispatch(1)
+    spread_line(nz - 1)
+    compute(0)
+    forward(1)
+    finish(0)
+    compute(1)
+    for step in range(2, nz):
+        dispatch(step)
+        finish(step - 1)
+        forward(step)
+        compute(step)
+        expand(step - 1)
+    finish(nz - 1)
+    expand(nz - 1)
+    total = expand(0)
+    for step in range(1, nz):
+        copies["home", step].wait_recv()
+        total += partial[1, step - 1].astype(jnp.float32)
+    out[...] = total.astype(out.dtype)
+    for copy in copies.values():
+        copy.wait_send()
+
+
+def expert_lines(tokens, routes, route_weights, w_gate, w_up, w_down):
+    tok, width = tokens.shape
+    topk = routes.shape[1]
+    halves = lax.axis_size("ep")
+    experts = halves // 2
+    nz = halves // 8
+    cap = tok * topk * 4 // (3 * experts)
+    units = w_gate.shape[2]
+    match = routes[None, :, :] == jnp.arange(experts, dtype=jnp.int32)[:, None, None]
+    routed = jnp.any(match, axis=2)
+    factor = jnp.sum(jnp.where(match, route_weights[None, :, :], 0.0), axis=2)
+    earlier = jnp.triu(jnp.ones((tok, tok), jnp.bfloat16), 1)
+    slot = jnp.dot(routed.astype(jnp.bfloat16), earlier, preferred_element_type=jnp.float32)
+    plan = jnp.concatenate([jnp.where(routed, slot, -1.0), factor], axis=0)
+    vmem, anywhere = pl.BlockSpec(memory_space=pltpu.VMEM), pl.BlockSpec(memory_space=pl.ANY)
+    dma = pltpu.SemaphoreType.DMA
+    half_type = jnp.bfloat16
+    return pl.pallas_call(
+        functools.partial(experts_kernel, nz, cap),
+        out_shape=jax.ShapeDtypeStruct((tok, width), half_type),
+        in_specs=[vmem, vmem, anywhere, anywhere, anywhere],
+        out_specs=vmem,
+        scratch_shapes=[
+            pltpu.VMEM((nz, 2 * experts, tok), jnp.float32),
+            pltpu.VMEM((nz - 1, tok, width), half_type),
+            pltpu.VMEM((nz, 3, cap, width), half_type),
+            pltpu.VMEM((nz, 8 * cap, width), half_type),
+            pltpu.VMEM((8 * cap, units), half_type),
+            pltpu.VMEM((nz, 8 * cap, width), half_type),
+            pltpu.VMEM((nz, 4 * cap, width), half_type),
+            pltpu.VMEM((nz, 4 * cap, width), half_type),
+            pltpu.VMEM((2, nz - 1, tok, width), half_type),
+            pltpu.VMEM((width, units), half_type),
+            pltpu.VMEM((width, units), half_type),
+            pltpu.VMEM((units, width), half_type),
+            dma((3,)), dma((nz,)), dma((nz,)), dma((nz,)), dma((nz,)),
+            dma((nz, 4)), dma((nz, 4)), dma((nz, 4)), dma((nz, 4)),
+            dma((nz,)), dma((nz,)), dma((nz, 4)), dma((nz, 4)), dma((nz,)), dma((nz,)),
+        ],
+        compiler_params=pltpu.CompilerParams(
+            collective_id=0, has_side_effects=True, vmem_limit_bytes=63 << 20
+        ),
+    )(tokens, plan, w_gate[0], w_up[0], w_down[0])
+
+
 def shards(
     tokens, routes, route_weights, w_gate, w_up, w_down, queries, key_cache, value_cache, lengths
 ):
+    if lax.axis_size("kv") == 1:
+        moe_out = expert_lines(tokens, routes, route_weights, w_gate, w_up, w_down)
+        return (moe_out, attend(queries, key_cache, value_cache, lengths))
     tok = tokens.shape[0]
     width = tokens.shape[1]
     topk = routes.shape[1]

time: 582 us -> 181 us (0.31); the launches traced: 574 us -> 181 us
  blocking collectives: 234 us -> 0 us
  waiting for transfers between devices: 223 us -> 0 us
  Pallas kernels: 0 us -> 173 us
  local copies, waits for them, and re-layouts: 58.7 us -> 4.26 us
  matrix products: 32.9 us -> 0.84 us
  other arithmetic: 19.2 us -> 1.59 us
    all_to_all x1 -> x0, blocking collectives: 234 us -> none  [shards(): lax.all_to_all(jnp.repeat(outgoing, 2, axis=0), 'ep', split_axis=0, conca...]
    all_to_all x1 -> x0, waiting for transfers between devices: 223 us -> none  [shards(): lax.all_to_all(half_out, 'ep', split_axis=0, concat_axis=0, tiled=True)]
    pallas_call x0 -> x1, Pallas kernels: none -> 173 us  [expert_lines(): pl.pallas_call(functools.partial(experts_kernel, nz, cap), out_shape=jax....]
    gather x3 -> x0, local copies, waits for them, and re-layouts: 33.7 us -> none  [the longest x1 13.7 us: shards(): table[first_row].astype(jnp.float32)]
    dot_general x3 -> x1, matrix products: 32.2 us -> 0.13 us  [expert_lines(): jnp.dot(routed.astype(jnp.bfloat16), earlier, preferred_element_type=jnp....]
    add x1 -> x0, local copies, waits for them, and re-layouts: 9.24 us -> none  [shards(): table[first_row].astype(jnp.float32)]
    reduce_sum x2 -> x1, other arithmetic: 8.92 us -> 0.01 us  [expert_lines(): factor = jnp.sum(jnp.where(match, route_weights[None, :, :], 0.0), axis=2)]
    broadcast_in_dim x1 -> x0, local copies, waits for them, and re-layouts: 7.91 us -> none  [shards(): jnp.repeat(outgoing, 2, axis=0)]
  transfers between devices with their start and end apart: 1 -> 0, of which waited for: 1 -> 0; matrix products, arithmetic and copies ran while one was open for 0% -> 0% of each run, Pallas kernels for 0% -> 0%
where the time goes in v3:
time: 181 us
  Pallas kernels  173 us (96%)
  local copies, waits for them, and re-layouts  4.26 us (2%)
    pallas_call x1, Pallas kernels, expert_lines(): pl.pallas_call(functools.partial(experts_kernel, nz, cap), out_shape=jax....  173 us

profile of v3, /device:TPU:9, one launch (start us, length us, event | category | flops | bytes accessed | tf_op | source)
XLA Modules:
  0.0 181.0 jit_solution(6649588038809951766)
XLA Ops:
  0.6 0.0 copy-start
  0.6 0.0 copy-start.1
  0.7 0.0 copy-start.2
  1.4 1.3 reshape.69
  2.8 0.7 reduce.4
  3.5 0.4 fusion.4
  3.9 0.2 fusion.16
  4.1 0.0 copy-done
  4.1 0.3 reshape.70
  4.4 0.3 fusion.5
  4.7 0.6 convert_element_type.21
  5.4 0.0 copy-done.1
  5.4 0.1 convolution_select_fusion
  5.5 0.0 copy-done.2
  5.5 0.6 pad_maximum_fusion.plan
  6.1 172.9 %shard_map.113 = bf16[128,2560]{1,0:T(8,128)(2,1)} custom-call(bf16[128,2560]{1,0:T(8,128)(2,1)} %tokens.1, f32[32,128]{1,0:T(8,128)} %pad_maximum_fusion.plan, bf16[2560,768]{1,0:T(8,128)(2,1)} %bitcast.9, bf16[2560,768]{1,0:T(8,128)(2,1)} %bitcast.10, bf16[768,2560]{1,0:T(8,128)(2,1)} %bitcast.11), custom_call_target="tpu_custom_call" | custom-call | tf_op jit(solution)/shard_map/pallas_call | solution.py:288
  179.0 2.0 %copy.28 = bf16[128,2560]{1,0:T(8,128)(2,1)} copy(bf16[128,2560]{1,0:T(8,128)(2,1)} %shard_map.113) | data formatting | bytes 1310720
  (4 shorter events, 0.0 us)
Async XLA Ops:
  0.6 3.5 %copy-start = (bf16[1,1024,512]{2,1,0:T(8,128)(2,1)S(1)}, bf16[1,1024,512]{2,1,0:T(8,128)(2,1)}, u32[]{:S(2)}) copy-start(bf16[1,1024,512]{2,1,0:T(8,128)(2,1)} %param.18) | copy-start | bytes 3145732
  0.6 4.7 %copy-start.1 = (s32[128,6]{0,1:T(8,128)S(1)}, s32[128,6]{0,1:T(8,128)}, u32[]{:S(2)}) copy-start(s32[128,6]{0,1:T(8,128)} %param.11) | copy-start | bytes 9220
  0.7 4.9 %copy-start.2 = (f32[128,6]{0,1:T(8,128)S(1)}, f32[128,6]{0,1:T(8,128)}, u32[]{:S(2)}) copy-start(f32[128,6]{0,1:T(8,128)} %param.12) | copy-start | bytes 9220

commit v4 on v3

--- a/solution.py
+++ b/solution.py
@@ -238,27 +238,31 @@
         for i, (source, target) in enumerate(((w_gate, gate_w), (w_up, up_w), (w_down, down_w)))
     ]
     greet(plane[1:] + [partner] + peers[1:])
-    for step in range(1, nz - 1):
+    order = [nz // 2] + [step for step in range(1, nz) if step != nz // 2]
+    for step in order[:-1]:
         spread_line(step)
     for copy in weights:
         copy.start()
     plans[0] = plan[...]
     dispatch(0)
     forward(0)
-    dispatch(1)
-    spread_line(nz - 1)
+    spread_line(order[-1])
     compute(0)
-    forward(1)
+    for step in order[:-1]:
+        dispatch(step)
+    for turn, step in enumerate(order):
+        forward(step)
+        if turn == 1:
+            dispatch(order[-1])
+        if turn:
+            finish(order[turn - 1])
+        if turn > 1:
+            expand(order[turn - 2])
+        compute(step)
+    finish(order[-1])
     finish(0)
-    compute(1)
-    for step in range(2, nz):
-        dispatch(step)
-        finish(step - 1)
-        forward(step)
-        compute(step)
-        expand(step - 1)
-    finish(nz - 1)
-    expand(nz - 1)
+    expand(order[-2])
+    expand(order[-1])
     total = expand(0)
     for step in range(1, nz):
         copies["home", step].wait_recv()

time: 181 us -> 163 us (0.901)
  Pallas kernels: 173 us -> 155 us
    pallas_call x1, Pallas kernels: 173 us -> 155 us  [expert_lines(): pl.pallas_call(functools.partial(experts_kernel, nz, cap), out_shape=jax....]
where the time goes in v4:
time: 163 us
  Pallas kernels  155 us (95%)
  local copies, waits for them, and re-layouts  4.26 us (3%)
    pallas_call x1, Pallas kernels, expert_lines(): pl.pallas_call(functools.partial(experts_kernel, nz, cap), out_shape=jax....  155 us

profile of v4, /device:TPU:9, one launch (start us, length us, event | category | flops | bytes accessed | tf_op | source)
XLA Modules:
  0.0 163.1 jit_solution(14591700391809830179)
XLA Ops:
  0.6 0.0 copy-start
  0.6 0.0 copy-start.1
  0.7 0.0 copy-start.2
  1.4 1.3 reshape.69
  2.8 0.7 reduce.4
  3.5 0.4 fusion.4
  3.9 0.2 fusion.16
  4.1 0.0 copy-done
  4.1 0.3 reshape.70
  4.4 0.3 fusion.5
  4.7 0.6 convert_element_type.21
  5.4 0.0 copy-done.1
  5.4 0.1 convolution_select_fusion
  5.5 0.0 copy-done.2
  5.5 0.6 pad_maximum_fusion.plan
  6.1 155.0 %shard_map.113 = bf16[128,2560]{1,0:T(8,128)(2,1)} custom-call(bf16[128,2560]{1,0:T(8,128)(2,1)} %tokens.1, f32[32,128]{1,0:T(8,128)} %pad_maximum_fusion.plan, bf16[2560,768]{1,0:T(8,128)(2,1)} %bitcast.9, bf16[2560,768]{1,0:T(8,128)(2,1)} %bitcast.10, bf16[768,2560]{1,0:T(8,128)(2,1)} %bitcast.11), custom_call_target="tpu_custom_call" | custom-call | tf_op jit(solution)/shard_map/pallas_call | solution.py:292
  161.1 2.0 %copy.28 = bf16[128,2560]{1,0:T(8,128)(2,1)} copy(bf16[128,2560]{1,0:T(8,128)(2,1)} %shard_map.113) | data formatting | bytes 1310720
  (4 shorter events, 0.0 us)
Async XLA Ops:
  0.6 3.5 %copy-start = (bf16[1,1024,512]{2,1,0:T(8,128)(2,1)S(1)}, bf16[1,1024,512]{2,1,0:T(8,128)(2,1)}, u32[]{:S(2)}) copy-start(bf16[1,1024,512]{2,1,0:T(8,128)(2,1)} %param.18) | copy-start | bytes 3145732
  0.6 4.7 %copy-start.1 = (s32[128,6]{0,1:T(8,128)S(1)}, s32[128,6]{0,1:T(8,128)}, u32[]{:S(2)}) copy-start(s32[128,6]{0,1:T(8,128)} %param.11) | copy-start | bytes 9220
  0.7 4.9 %copy-start.2 = (f32[128,6]{0,1:T(8,128)S(1)}, f32[128,6]{0,1:T(8,128)}, u32[]{:S(2)}) copy-start(f32[128,6]{0,1:T(8,128)} %param.12) | copy-start | bytes 9220
